TPU v7x, 512 devices: a whole 4x8x8 slice. The times are simulated.
512 devices in a mesh: dp: 128 (over z, y, core), tensor: 4 (over x).
Axes of the slice: x: 4, y: 8, z: 8, core: 2. Of those that a mesh axis runs over, the one named last changes fastest.
Arguments:
- hidden: bfloat16 [65536, 1024], P('dp', 'tensor'), may hold values from -24 to 24
- gain: float32 [1024], replicated, may hold values from 0.5 to 1.5
- head_weight: bfloat16 [1024, 25600], P(None, ('tensor', 'dp')), may hold values from -6 to 6
- targets: int32 [65536], P('dp'), may hold values from 0 to 25599
- row_count: int32 [128], P('dp'), may hold values from 64 to 512, as said below
- dest: int32 [65536], P('dp'), may hold values from 0 to 65535, as said below
Outputs:
- logprob: float32 [65536], P('dp')
- entropy: float32 [65536], P('dp')
Inputs may be any that keep to these rules, and one draw needn't show every extreme that they name: Each device's live slots are its first row_count ones; at least one device is full. dest is a permutation. Slot results of device s go to device dest // 512; every device sends exactly 4 results to every device, those from device s fill positions s * 4 to (s + 1) * 4 - 1 of the receiver's block, in the order of their position in the sender's slots sorted by destination.
All inputs are finite; a program needn't handle non-finite values.
Results may differ from a plain program's by a relative error of at most 0.0062.
Values may be sent and summed in bfloat16 or wider, within the bound.
A program may use at most 128 MiB of HBM per device.

v0:
```python
import jax
import jax.numpy as jnp
from jax import lax
from jax.sharding import Mesh, PartitionSpec as P


def stats_of(logits_t, wanted):
    top = jnp.max(logits_t, axis=0)
    weights = jnp.exp(logits_t - top[None, :])
    mass = jnp.sum(weights, axis=0)
    moment = jnp.sum(weights * logits_t, axis=0)
    ids = lax.broadcasted_iota(jnp.int32, logits_t.shape, 0)
    picked = jnp.sum(jnp.where(ids == wanted[None, :], logits_t, 0.0), axis=0)
    return jnp.stack([top, mass, moment, picked])


def merge(parts):
    top = jnp.max(parts[:, 0], axis=0)
    factor = jnp.exp(parts[:, 0] - top[None])
    mass = jnp.sum(parts[:, 1] * factor, axis=0)
    moment = jnp.sum(parts[:, 2] * factor, axis=0)
    return (top, mass, moment, jnp.sum(parts[:, 3], axis=0))


def body(hidden, gain, head_weight, targets, row_count, dest):
    rows = hidden.shape[0]
    cols = head_weight.shape[1]
    padded = -(-cols // 8) * 8
    groups = lax.axis_size("zy") * 2
    tensors = lax.axis_size("tensor")
    core = lax.axis_index("core")
    mine = lax.axis_index("tensor")
    swap = [(0, 1), (1, 0)]
    spread = jnp.pad(head_weight.T, ((0, padded - cols), (0, 0)))
    piece = lax.all_gather(spread, "zy", axis=0, tiled=True)
    shards = [hidden]
    for step in range(1, tensors):
        shards.append(
            lax.ppermute(hidden, "tensor", [((i + step) % tensors, i) for i in range(tensors)])
        )
    own = jnp.stack(shards)
    other = lax.ppermute(own, "core", swap)
    both = jnp.concatenate([own, other], axis=1).astype(jnp.float32)
    power = jnp.sum(both * both, axis=(0, 2)) / (tensors * hidden.shape[1])
    scale = lax.rsqrt(power + 1e-06)
    gains = jnp.roll(gain.reshape(tensors, -1), -mine, axis=0)
    turned = (both * scale[None, :, None] * gains[:, None, :]).astype(jnp.bfloat16)
    ordered = jnp.roll(turned, mine, axis=0)
    normed = jnp.moveaxis(ordered, 0, 1).reshape(2 * rows, -1)
    wanted = jnp.concatenate([targets, lax.ppermute(targets, "core", swap)])
    local = wanted - mine * (cols * groups)
    device = local // cols
    ok = (local >= 0) & (device < groups) & (device % 2 == core)
    slot = jnp.where(ok, device // 2 * padded + local % cols, -1)
    logits = lax.dot_general(
        piece, normed, (((1,), (1,)), ((), ())), preferred_element_type=jnp.float32
    )
    ids = lax.broadcasted_iota(jnp.int32, logits.shape, 0)
    logits = jnp.where(ids % padded < cols, logits, -1e30)
    stats = stats_of(logits, slot)
    theirs = lax.ppermute(stats[:, rows:], "core", swap)
    pair = jnp.stack(merge(jnp.stack([stats[:, :rows], theirs])))
    top, mass, moment, picked = merge(lax.all_gather(pair, "tensor", axis=0))
    live = jnp.arange(rows, dtype=jnp.int32) < row_count[0]
    lse = top + jnp.log(mass)
    value_lp = jnp.where(live, picked - lse, 0.0)
    value_ent = jnp.where(live, lse - moment / mass, 0.0)
    share = rows // groups
    rank = dest // rows * share + dest % share
    hit = lax.broadcasted_iota(jnp.int32, (rows, rows), 0) == rank[None, :]
    sent = [
        jnp.sum(jnp.where(hit, v[None, :], 0.0), axis=1).reshape(groups, share)
        for v in (value_lp, value_ent)
    ]
    got = lax.all_to_all(jnp.concatenate(sent, axis=1), ("zy", "core"), 0, 0, tiled=True)
    return (got[:, :share].reshape(rows), got[:, share:].reshape(rows))


def solution(mesh):
    dp, tensor = mesh.devices.shape
    fine = Mesh(mesh.devices.reshape(dp // 2, 2, tensor), ("zy", "core", "tensor"))
    group = ("zy", "core")
    in_specs = (
        P(group, "tensor"),
        P(),
        P(None, ("tensor", "zy", "core")),
        P(group),
        P(group),
        P(group),
    )
    return jax.shard_map(
        body, mesh=fine, in_specs=in_specs, out_specs=(P(group), P(group)), check_vma=False
    )
```

profile of v0, /device:TPU:1, one launch (start us, length us, event | category | flops | bytes accessed | tf_op | source)
XLA Modules:
  0.0 172.6 jit_solution(16111850264375092905)
XLA Ops:
  7.2 1.6 pad.4
  8.8 1.1 copy.31
  9.9 5.2 %collective-permute-start = (bf16[512,256]{0,1:T(8,128)(2,1)S(1)}, bf16[512,256]{0,1:T(8,128)(2,1)S(1)}, u32[]{:S(2)}, u32[]{:S(2)}) collective-permute-start(bf16[512,256]{0,1:T(8,128)(2,1)S(1)} %copy.31), channel_id=1, source_target_pairs={{1,0},{2,1},{3,2},{0,3},{5,4},{6,5},{7,6},{4,7},{9,8},{10,9},{11,1... | collective-permute-start | bytes 786440 | tf_op jit(solution)/shard_map/ppermute | solution.py:39
  15.1 2.4 %collective-permute-start.1 = (bf16[512,256]{0,1:T(8,128)(2,1)S(1)}, bf16[512,256]{0,1:T(8,128)(2,1)S(1)}, u32[]{:S(2)}, u32[]{:S(2)}) collective-permute-start(bf16[512,256]{0,1:T(8,128)(2,1)S(1)} %copy.31), channel_id=1, source_target_pairs={{2,0},{3,1},{0,2},{1,3},{6,4},{7,5},{4,6},{5,7},{10,8},{11,9},{8,1... | collective-permute-start | bytes 786440 | tf_op jit(solution)/shard_map/ppermute | solution.py:39
  17.5 2.5 %collective-permute-start.2 = (bf16[512,256]{0,1:T(8,128)(2,1)S(1)}, bf16[512,256]{0,1:T(8,128)(2,1)S(1)}, u32[]{:S(2)}, u32[]{:S(2)}) collective-permute-start(bf16[512,256]{0,1:T(8,128)(2,1)S(1)} %copy.31), channel_id=1, source_target_pairs={{3,0},{0,1},{1,2},{2,3},{7,4},{4,5},{5,6},{6,7},{11,8},{8,9},{9,10... | collective-permute-start | bytes 786440 | tf_op jit(solution)/shard_map/ppermute | solution.py:39
  20.1 3.7 %collective-permute-done.1 = bf16[512,256]{0,1:T(8,128)(2,1)S(1)} collective-permute-done((bf16[512,256]{0,1:T(8,128)(2,1)S(1)}, bf16[512,256]{0,1:T(8,128)(2,1)S(1)}, u32[]{:S(2)}, u32[]{:S(2)}) %collective-permute-start.1) | collective-permute-done | bytes 262176 | tf_op jit(solution)/shard_map/ppermute | solution.py:39
  23.8 4.7 %collective-permute-done.2 = bf16[512,256]{0,1:T(8,128)(2,1)S(1)} collective-permute-done((bf16[512,256]{0,1:T(8,128)(2,1)S(1)}, bf16[512,256]{0,1:T(8,128)(2,1)S(1)}, u32[]{:S(2)}, u32[]{:S(2)}) %collective-permute-start.2) | collective-permute-done | bytes 262176 | tf_op jit(solution)/shard_map/ppermute | solution.py:39
  28.6 6.2 %collective-permute-start.3 = (bf16[4,512,256]{1,2,0:T(8,128)(2,1)S(1)}, bf16[4,512,256]{1,2,0:T(8,128)(2,1)S(1)}, u32[]{:S(2)}, u32[]{:S(2)}) collective-permute-start(bf16[4,512,256]{1,2,0:T(8,128)(2,1)S(1)} %pad_maximum_fusion.1), channel_id=1, source_target_pairs={{0,4},{4,0},{1,5},{5,1},{2,6},{6,2},{3,7},{7,3},{8,12},{12,8},{9,1... | collective-permute-start | bytes 3145736 | tf_op jit(solution)/shard_map/ppermute | solution.py:42
  34.9 1.9 %collective-permute-start.4 = (s32[512]{0:T(512)}, s32[512]{0:T(512)S(1)}, u32[]{:S(2)}, u32[]{:S(2)}) collective-permute-start(s32[512]{0:T(512)} %param.9), channel_id=1, source_target_pairs={{0,4},{4,0},{1,5},{5,1},{2,6},{6,2},{3,7},{7,3},{8,12},{12,8},{9,1... | collective-permute-start | bytes 6152 | tf_op jit(solution)/shard_map/ppermute | solution.py:50
  36.8 0.7 reshape.120
  37.6 0.5 collective-permute-done.4
  38.2 0.7 fusion.21
  38.9 0.5 fusion.2
  39.4 0.6 fusion.4
  40.0 0.8 fusion.5
  40.8 69.9 %all-gather.4.cloned.1.call-done = bf16[3584,1024]{1,0:T(8,128)(2,1)} async-done(((bf16[56,1024]{1,0:T(8,128)(2,1)}), bf16[3584,1024]{1,0:T(8,128)(2,1)}) %all-gather.4.cloned.1.call-update) | async-done | bytes 7340048 | tf_op jit(solution)/shard_map/all_gather | solution.py:35
  110.7 10.5 %fusion.40 = (f32[1024]{0:T(1024)S(1)}, f32[3584,1024]{1,0:T(8,128)S(1)}) fusion(bf16[3584,1024]{1,0:T(8,128)(2,1)} %all-gather.4.cloned.1.call-done, bf16[1024,1024]{0,1:T(8,128)(2,1)S(1)} %bitcast.76, s32[3584]{0:T(1024)S(1)} %get-tuple-element.29, s32[3584]{0:T(1024)S(1)} %get-tuple-element.30, pred[3584]{0:T(1024)(128)(4,1)S(1)} %fusion.9), kind=kOutput, calls=%fused_computation.97 | convolution fusion | flops 7530871808 | bytes 24153600 | tf_op jit(solution)/shard_map/dot_general | solution.py:55
  121.1 4.8 %fusion = (f32[1024]{0:T(1024)S(1)}, f32[1024]{0:T(1024)S(1)}, f32[1024]{0:T(1024)S(1)}) fusion(f32[3584,1024]{1,0:T(8,128)S(1)} %get-tuple-element.28, f32[1024]{0:T(1024)S(1)} %get-tuple-element.27, s32[1024]{0:T(1024)S(1)} %fusion.21), kind=kLoop, calls=%fused_computation.4 | loop fusion | flops 25687040 | bytes 14700544 | tf_op jit(solution)/shard_map/reduce_sum | solution.py:10
  126.0 3.0 %collective-permute-start.5 = (f32[4,512]{1,0:T(4,128)S(1)}, f32[4,512]{1,0:T(4,128)S(1)}, u32[]{:S(2)}, u32[]{:S(2)}) collective-permute-start(f32[4,512]{1,0:T(4,128)S(1)} %get-tuple-element.24), channel_id=1, source_target_pairs={{0,4},{4,0},{1,5},{5,1},{2,6},{6,2},{3,7},{7,3},{8,12},{12,8},{9,1... | collective-permute-start | bytes 24584 | tf_op jit(solution)/shard_map/ppermute | solution.py:61
  130.0 9.3 %all-gather.1 = f32[4,4,512]{2,1,0:T(4,128)S(1)} all-gather(f32[1,4,512]{2,1,0:T(4,128)S(1)} %maximum_bitcast_fusion), channel_id=2, replica_groups=mesh['zy'=64,'core'=2,'tensor'=4] {'tensor'}, dimensions={0}, use_global_device_ids=true | all-gather | bytes 40960 | tf_op jit(solution)/shard_map/all_gather | solution.py:63
  139.4 0.4 select_reduce_fusion.2
  140.1 24.2 %all_to_all.12 = f32[128,1,8]{2,1,0:T(1,128)S(1)} all-to-all(f32[128,1,8]{2,1,0:T(1,128)S(1)} %bitcast.78), channel_id=1, replica_groups=mesh['zy'=64,'core'=2,'tensor'=4] {'zy','core'}, dimensions={0} | all-to-all | bytes 8192 | tf_op jit(solution)/shard_map/all_to_all | solution.py:75
  164.4 0.7 reshape.124
  165.1 0.7 reshape.125
  (27 shorter events, 0.9 us)
Async XLA Ops:
  7.2 103.5 %all-gather.4.cloned.1.call-start = ((), (), s32[]{:S(2)}) async-start(), calls=%async_computation.1 | async-start | bytes 7454720 | tf_op jit(solution)/shard_map/all_gather | solution.py:35
  9.9 10.2 %collective-permute-start = (bf16[512,256]{0,1:T(8,128)(2,1)S(1)}, bf16[512,256]{0,1:T(8,128)(2,1)S(1)}, u32[]{:S(2)}, u32[]{:S(2)}) collective-permute-start(bf16[512,256]{0,1:T(8,128)(2,1)S(1)} %copy.31), channel_id=1, source_target_pairs={{1,0},{2,1},{3,2},{0,3},{5,4},{6,5},{7,6},{4,7},{9,8},{10,9},{11,1... | collective-permute-start | bytes 786440 | tf_op jit(solution)/shard_map/ppermute | solution.py:39
  15.1 8.7 %collective-permute-start.1 = (bf16[512,256]{0,1:T(8,128)(2,1)S(1)}, bf16[512,256]{0,1:T(8,128)(2,1)S(1)}, u32[]{:S(2)}, u32[]{:S(2)}) collective-permute-start(bf16[512,256]{0,1:T(8,128)(2,1)S(1)} %copy.31), channel_id=1, source_target_pairs={{2,0},{3,1},{0,2},{1,3},{6,4},{7,5},{4,6},{5,7},{10,8},{11,9},{8,1... | collective-permute-start | bytes 786440 | tf_op jit(solution)/shard_map/ppermute | solution.py:39
  17.5 11.0 %collective-permute-start.2 = (bf16[512,256]{0,1:T(8,128)(2,1)S(1)}, bf16[512,256]{0,1:T(8,128)(2,1)S(1)}, u32[]{:S(2)}, u32[]{:S(2)}) collective-permute-start(bf16[512,256]{0,1:T(8,128)(2,1)S(1)} %copy.31), channel_id=1, source_target_pairs={{3,0},{0,1},{1,2},{2,3},{7,4},{4,5},{5,6},{6,7},{11,8},{8,9},{9,10... | collective-permute-start | bytes 786440 | tf_op jit(solution)/shard_map/ppermute | solution.py:39
  28.6 10.2 %collective-permute-start.3 = (bf16[4,512,256]{1,2,0:T(8,128)(2,1)S(1)}, bf16[4,512,256]{1,2,0:T(8,128)(2,1)S(1)}, u32[]{:S(2)}, u32[]{:S(2)}) collective-permute-start(bf16[4,512,256]{1,2,0:T(8,128)(2,1)S(1)} %pad_maximum_fusion.1), channel_id=1, source_target_pairs={{0,4},{4,0},{1,5},{5,1},{2,6},{6,2},{3,7},{7,3},{8,12},{12,8},{9,1... | collective-permute-start | bytes 3145736 | tf_op jit(solution)/shard_map/ppermute | solution.py:42
  34.9 3.3 %collective-permute-start.4 = (s32[512]{0:T(512)}, s32[512]{0:T(512)S(1)}, u32[]{:S(2)}, u32[]{:S(2)}) collective-permute-start(s32[512]{0:T(512)} %param.9), channel_id=1, source_target_pairs={{0,4},{4,0},{1,5},{5,1},{2,6},{6,2},{3,7},{7,3},{8,12},{12,8},{9,1... | collective-permute-start | bytes 6152 | tf_op jit(solution)/shard_map/ppermute | solution.py:50
  121.1 7.9 %copy-start = (s32[512]{0:T(512)S(1)}, s32[512]{0:T(512)}, u32[]{:S(2)}) copy-start(s32[512]{0:T(512)} %param.11) | copy-start | bytes 6148
  126.0 3.9 %collective-permute-start.5 = (f32[4,512]{1,0:T(4,128)S(1)}, f32[4,512]{1,0:T(4,128)S(1)}, u32[]{:S(2)}, u32[]{:S(2)}) collective-permute-start(f32[4,512]{1,0:T(4,128)S(1)} %get-tuple-element.24), channel_id=1, source_target_pairs={{0,4},{4,0},{1,5},{5,1},{2,6},{6,2},{3,7},{7,3},{8,12},{12,8},{9,1... | collective-permute-start | bytes 24584 | tf_op jit(solution)/shard_map/ppermute | solution.py:61
Sparse Core Ops, SparseCore 0:
  11.0 99.6 all-gather.3
where the time goes:
time: 173 us
  waiting for transfers between devices  79 us (46%)
  blocking collectives  33.6 us (19%)
  starting transfers between devices  21.4 us (12%)
  between operations  14.9 us (9%)
  matrix products  10.5 us (6%)
  other arithmetic  8.21 us (5%)
  local copies, waits for them, and re-layouts  5.03 us (3%)
    all_gather x1, waiting for transfers between devices, body(): piece = lax.all_gather(spread, 'zy', axis=0, tiled=True)  69.9 us
    all_to_all x1, blocking collectives, body(): lax.all_to_all(jnp.concatenate(sent, axis=1), ('zy', 'core'), 0, 0, tiled...  24.2 us
    dot_general x1, matrix products, body(): lax.dot_general(piece, normed, (((1,), (1,)), ((), ())), preferred_elemen...  10.5 us
    ppermute x3, starting transfers between devices, body(): lax.ppermute(hidden, 'tensor', [((i + step) % tensors, i) for i in range(...  10.1 us
    all_gather x1, blocking collectives, body(): top, mass, moment, picked = merge(lax.all_gather(pair, 'tensor', axis=0))  9.34 us
    ppermute x3, waiting for transfers between devices, body(): lax.ppermute(hidden, 'tensor', [((i + step) % tensors, i) for i in range(...  8.43 us
    ppermute x1, starting transfers between devices, body(): other = lax.ppermute(own, 'core', swap)  6.25 us
    reduce_sum x1, other arithmetic, stats_of(): mass = jnp.sum(weights, axis=0)  4.82 us
  transfers between devices with their start and end apart: 7, of which 5 were waited for; matrix products, arithmetic and copies ran while one was open for 3% of the time, Pallas kernels for 0%

commit v1 on v0

--- a/solution.py
+++ b/solution.py
@@ -32,7 +32,9 @@
     mine = lax.axis_index("tensor")
     swap = [(0, 1), (1, 0)]
     spread = jnp.pad(head_weight.T, ((0, padded - cols), (0, 0)))
-    piece = lax.all_gather(spread, "zy", axis=0, tiled=True)
+    piece = jnp.concatenate(
+        lax.all_to_all(jnp.stack([spread] * lax.axis_size("zy")), "zy", 0, 0), axis=0
+    )
     shards = [hidden]
     for step in range(1, tensors):
         shards.append(

time: 173 us -> 334 us (1.93)
  waiting for transfers between devices: 79 us -> 181 us
  blocking collectives: 33.6 us -> 92 us
  between operations: 14.9 us -> 1.59 us
  starting transfers between devices: 21.4 us -> 34.6 us
    all_to_all x0 -> x1, waiting for transfers between devices: none -> 168 us  [body(): lax.all_to_all(jnp.stack([spread] * lax.axis_size('zy')), 'zy', 0, 0)]
    all_gather x1 -> x0, waiting for transfers between devices: 69.9 us -> none  [body(): piece = lax.all_gather(spread, 'zy', axis=0, tiled=True)]
    all_to_all x1, blocking collectives: 24.2 us -> 82.7 us  [body(): lax.all_to_all(jnp.concatenate(sent, axis=1), ('zy', 'core'), 0, 0, tiled...]
    all_to_all x0 -> x1, starting transfers between devices: none -> 17.5 us  [body(): lax.all_to_all(jnp.stack([spread] * lax.axis_size('zy')), 'zy', 0, 0)]
    another operation x0 -> x1, local copies, waits for them, and re-layouts: none -> 3.96 us  [body(): jnp.stack([spread] * lax.axis_size('zy'))]
    ppermute x3, waiting for transfers between devices: 8.43 us -> 12.4 us  [body(): lax.ppermute(hidden, 'tensor', [((i + step) % tensors, i) for i in range(...]
    ppermute x1, starting transfers between devices: 6.25 us -> 2.31 us  [body(): other = lax.ppermute(own, 'core', swap)]
  transfers between devices with their start and end apart: 7 -> 7, of which waited for: 5 -> 6; matrix products, arithmetic and copies ran while one was open for 3% -> 1% of each run, Pallas kernels for 0% -> 0%
where the time goes in v1:
time: 334 us
  waiting for transfers between devices  181 us (54%)
  blocking collectives  92 us (28%)
  starting transfers between devices  34.6 us (10%)
  matrix products  10.5 us (3%)
  other arithmetic  7.53 us (2%)
  local copies, waits for them, and re-layouts  6.72 us (2%)
    all_to_all x1, waiting for transfers between devices, body(): lax.all_to_all(jnp.stack([spread] * lax.axis_size('zy')), 'zy', 0, 0)  168 us
    all_to_all x1, blocking collectives, body(): lax.all_to_all(jnp.concatenate(sent, axis=1), ('zy', 'core'), 0, 0, tiled...  82.7 us
    all_to_all x1, starting transfers between devices, body(): lax.all_to_all(jnp.stack([spread] * lax.axis_size('zy')), 'zy', 0, 0)  17.5 us
    ppermute x3, waiting for transfers between devices, body(): lax.ppermute(hidden, 'tensor', [((i + step) % tensors, i) for i in range(...  12.4 us
    dot_general x1, matrix products, body(): lax.dot_general(piece, normed, (((1,), (1,)), ((), ())), preferred_elemen...  10.5 us
    all_gather x1, blocking collectives, body(): top, mass, moment, picked = merge(lax.all_gather(pair, 'tensor', axis=0))  9.39 us
    ppermute x3, starting transfers between devices, body(): lax.ppermute(hidden, 'tensor', [((i + step) % tensors, i) for i in range(...  9.33 us
  transfers between devices with their start and end apart: 7, of which 6 were waited for; matrix products, arithmetic and copies ran while one was open for 1% of the time, Pallas kernels for 0%

profile of v1, /device:TPU:1, one launch (start us, length us, event | category | flops | bytes accessed | tf_op | source)
XLA Modules:
  0.0 334.0 jit_solution(12942541843424387394)
XLA Ops:
  0.6 0.9 pad.4
  1.5 4.0 %stack.38 = bf16[64,56,1024]{2,1,0:T(8,128)(2,1)} broadcast(bf16[56,1024]{1,0:T(8,128)(2,1)S(1)} %pad.4), dimensions={1,2} | broadcast | bytes 7454720 | tf_op jit(solution)/shard_map/stack | solution.py:36
  5.5 17.5 %all-to-all-start = ((bf16[64,56,1024]{2,1,0:T(8,128)(2,1)}), bf16[64,56,1024]{2,1,0:T(8,128)(2,1)}, u32[]{:S(2)}, u32[]{:S(2)}) async-start(bf16[64,56,1024]{2,1,0:T(8,128)(2,1)} %stack.38), calls=%async_computation | async-start | bytes 14680064 | tf_op jit(solution)/shard_map/all_to_all | solution.py:36
  23.2 4.4 %collective-permute-start = (bf16[512,256]{0,1:T(8,128)(2,1)S(1)}, bf16[512,256]{0,1:T(8,128)(2,1)S(1)}, u32[]{:S(2)}, u32[]{:S(2)}) collective-permute-start(bf16[512,256]{0,1:T(8,128)(2,1)S(1)} %copy.31), channel_id=1, source_target_pairs={{1,0},{2,1},{3,2},{0,3},{5,4},{6,5},{7,6},{4,7},{9,8},{10,9},{11,1... | collective-permute-start | bytes 786440 | tf_op jit(solution)/shard_map/ppermute | solution.py:41
  27.6 2.4 collective-permute-start.1
  30.0 2.5 collective-permute-start.2
  32.5 0.5 collective-permute-done
  33.0 4.7 %collective-permute-done.1 = bf16[512,256]{0,1:T(8,128)(2,1)S(1)} collective-permute-done((bf16[512,256]{0,1:T(8,128)(2,1)S(1)}, bf16[512,256]{0,1:T(8,128)(2,1)S(1)}, u32[]{:S(2)}, u32[]{:S(2)}) %collective-permute-start.1) | collective-permute-done | bytes 262176 | tf_op jit(solution)/shard_map/ppermute | solution.py:41
  37.7 7.2 %collective-permute-done.2 = bf16[512,256]{0,1:T(8,128)(2,1)S(1)} collective-permute-done((bf16[512,256]{0,1:T(8,128)(2,1)S(1)}, bf16[512,256]{0,1:T(8,128)(2,1)S(1)}, u32[]{:S(2)}, u32[]{:S(2)}) %collective-permute-start.2) | collective-permute-done | bytes 262176 | tf_op jit(solution)/shard_map/ppermute | solution.py:41
  45.0 2.3 collective-permute-start.3
  47.4 2.0 collective-permute-start.4
  49.5 0.9 collective-permute-done.4
  50.5 0.5 fusion.2
  51.0 0.6 fusion.4
  51.6 0.8 fusion.5
  52.4 167.6 %all-to-all-done = bf16[64,56,1024]{2,1,0:T(8,128)(2,1)} async-done(((bf16[64,56,1024]{2,1,0:T(8,128)(2,1)}), bf16[64,56,1024]{2,1,0:T(8,128)(2,1)}, u32[]{:S(2)}, u32[]{:S(2)}) %all-to-all-start) | async-done | bytes 7340064 | tf_op jit(solution)/shard_map/all_to_all | solution.py:36
  219.9 10.5 %fusion.40 = (f32[1024]{0:T(1024)S(1)}, f32[3584,1024]{1,0:T(8,128)S(1)}) fusion(bf16[3584,1024]{1,0:T(8,128)(2,1)} %bitcast.2, bf16[1024,1024]{0,1:T(8,128)(2,1)S(1)} %bitcast.77, s32[3584]{0:T(1024)S(1)} %get-tuple-element.29, s32[3584]{0:T(1024)S(1)} %get-tuple-element.30, pred[3584]{0:T(1024)(128)(4,1)S(1)} %fusion.9), kind=kOutput, calls=%fused_computation.97 | convolution fusion | flops 7530871808 | bytes 24153600 | tf_op jit(solution)/shard_map/dot_general | solution.py:57
  230.4 4.8 %fusion = (f32[1024]{0:T(1024)S(1)}, f32[1024]{0:T(1024)S(1)}, f32[1024]{0:T(1024)S(1)}) fusion(f32[3584,1024]{1,0:T(8,128)S(1)} %get-tuple-element.28, f32[1024]{0:T(1024)S(1)} %get-tuple-element.27, s32[1024]{0:T(1024)S(1)} %fusion.21), kind=kLoop, calls=%fused_computation.4 | loop fusion | flops 25687040 | bytes 14700544 | tf_op jit(solution)/shard_map/reduce_sum | solution.py:10
  235.3 3.5 %collective-permute-start.5 = (f32[4,512]{1,0:T(4,128)S(1)}, f32[4,512]{1,0:T(4,128)S(1)}, u32[]{:S(2)}, u32[]{:S(2)}) collective-permute-start(f32[4,512]{1,0:T(4,128)S(1)} %get-tuple-element.24), channel_id=1, source_target_pairs={{0,4},{4,0},{1,5},{5,1},{2,6},{6,2},{3,7},{7,3},{8,12},{12,8},{9,1... | collective-permute-start | bytes 24584 | tf_op jit(solution)/shard_map/ppermute | solution.py:63
  239.7 9.4 %all-gather.1 = f32[4,4,512]{2,1,0:T(4,128)S(1)} all-gather(f32[1,4,512]{2,1,0:T(4,128)S(1)} %maximum_bitcast_fusion), channel_id=2, replica_groups=mesh['zy'=64,'core'=2,'tensor'=4] {'tensor'}, dimensions={0}, use_global_device_ids=true | all-gather | bytes 40960 | tf_op jit(solution)/shard_map/all_gather | solution.py:65
  249.2 0.4 select_reduce_fusion.2
  249.9 82.7 %all_to_all.17 = f32[128,1,8]{2,1,0:T(1,128)S(1)} all-to-all(f32[128,1,8]{2,1,0:T(1,128)S(1)} %bitcast.79), channel_id=1, replica_groups=mesh['zy'=64,'core'=2,'tensor'=4] {'zy','core'}, dimensions={0} | all-to-all | bytes 8192 | tf_op jit(solution)/shard_map/all_to_all | solution.py:77
  332.6 0.7 reshape.130
  333.3 0.7 reshape.131
  (33 shorter events, 1.1 us)
Async XLA Ops:
  5.5 17.5 %copy-start = (bf16[512,256]{1,0:T(8,128)(2,1)S(1)}, bf16[512,256]{1,0:T(8,128)(2,1)}, u32[]{:S(2)}) copy-start(bf16[512,256]{1,0:T(8,128)(2,1)} %param.6) | copy-start | bytes 786436
  5.5 41.8 %copy-start.3 = (s32[512]{0:T(512)S(1)}, s32[512]{0:T(512)}, u32[]{:S(2)}) copy-start(s32[512]{0:T(512)} %param.9) | copy-start | bytes 6148
  5.5 43.9 %copy-start.1 = (f32[1024]{0:T(1024)S(1)}, f32[1024]{0:T(1024)}, u32[]{:S(2)}) copy-start(f32[1024]{0:T(1024)} %param.7) | copy-start | bytes 12292
  5.5 214.4 %all-to-all-start = ((bf16[64,56,1024]{2,1,0:T(8,128)(2,1)}), bf16[64,56,1024]{2,1,0:T(8,128)(2,1)}, u32[]{:S(2)}, u32[]{:S(2)}) async-start(bf16[64,56,1024]{2,1,0:T(8,128)(2,1)} %stack.38), calls=%async_computation | async-start | bytes 14680064 | tf_op jit(solution)/shard_map/all_to_all | solution.py:36
  23.2 9.9 %collective-permute-start = (bf16[512,256]{0,1:T(8,128)(2,1)S(1)}, bf16[512,256]{0,1:T(8,128)(2,1)S(1)}, u32[]{:S(2)}, u32[]{:S(2)}) collective-permute-start(bf16[512,256]{0,1:T(8,128)(2,1)S(1)} %copy.31), channel_id=1, source_target_pairs={{1,0},{2,1},{3,2},{0,3},{5,4},{6,5},{7,6},{4,7},{9,8},{10,9},{11,1... | collective-permute-start | bytes 786440 | tf_op jit(solution)/shard_map/ppermute | solution.py:41
  27.6 10.2 %collective-permute-start.1 = (bf16[512,256]{0,1:T(8,128)(2,1)S(1)}, bf16[512,256]{0,1:T(8,128)(2,1)S(1)}, u32[]{:S(2)}, u32[]{:S(2)}) collective-permute-start(bf16[512,256]{0,1:T(8,128)(2,1)S(1)} %copy.31), channel_id=1, source_target_pairs={{2,0},{3,1},{0,2},{1,3},{6,4},{7,5},{4,6},{5,7},{10,8},{11,9},{8,1... | collective-permute-start | bytes 786440 | tf_op jit(solution)/shard_map/ppermute | solution.py:41
  30.0 14.9 %collective-permute-start.2 = (bf16[512,256]{0,1:T(8,128)(2,1)S(1)}, bf16[512,256]{0,1:T(8,128)(2,1)S(1)}, u32[]{:S(2)}, u32[]{:S(2)}) collective-permute-start(bf16[512,256]{0,1:T(8,128)(2,1)S(1)} %copy.31), channel_id=1, source_target_pairs={{3,0},{0,1},{1,2},{2,3},{7,4},{4,5},{5,6},{6,7},{11,8},{8,9},{9,10... | collective-permute-start | bytes 786440 | tf_op jit(solution)/shard_map/ppermute | solution.py:41
  45.0 5.4 %collective-permute-start.3 = (bf16[4,512,256]{1,2,0:T(8,128)(2,1)S(1)}, bf16[4,512,256]{1,2,0:T(8,128)(2,1)S(1)}, u32[]{:S(2)}, u32[]{:S(2)}) collective-permute-start(bf16[4,512,256]{1,2,0:T(8,128)(2,1)S(1)} %pad_maximum_fusion.1), channel_id=1, source_target_pairs={{0,4},{4,0},{1,5},{5,1},{2,6},{6,2},{3,7},{7,3},{8,12},{12,8},{9,1... | collective-permute-start | bytes 3145736 | tf_op jit(solution)/shard_map/ppermute | solution.py:44
  47.4 3.1 collective-permute-start.4
  230.4 8.4 %copy-start.2 = (s32[512]{0:T(512)S(1)}, s32[512]{0:T(512)}, u32[]{:S(2)}) copy-start(s32[512]{0:T(512)} %param.11) | copy-start | bytes 6148
  235.3 4.3 %collective-permute-start.5 = (f32[4,512]{1,0:T(4,128)S(1)}, f32[4,512]{1,0:T(4,128)S(1)}, u32[]{:S(2)}, u32[]{:S(2)}) collective-permute-start(f32[4,512]{1,0:T(4,128)S(1)} %get-tuple-element.24), channel_id=1, source_target_pairs={{0,4},{4,0},{1,5},{5,1},{2,6},{6,2},{3,7},{7,3},{8,12},{12,8},{9,1... | collective-permute-start | bytes 24584 | tf_op jit(solution)/shard_map/ppermute | solution.py:63
